TPU v7x, 256 devices: a whole 4x4x8 slice. The times are simulated.
256 devices in a mesh: span: 64 (over y_hi, x, z), rows: 4 (over y_lo, core).
Axes of the slice: x: 4, y: 4 (y_hi: 2, y_lo: 2; y = y_hi * 2 + y_lo), z: 8, core: 2. Of those that a mesh axis runs over, the one named last changes fastest.
Arguments:
- pressure_source: float32 [256, 128, 1024], P('span', 'rows'), may hold values from -6 to 6
- geometry: float32 [64, 3, 128, 1024], P('span', None, 'rows'), may hold values from 0.1 to 1
- owner: int32 [1], replicated, may hold values from 0 to 63
Outputs:
- pressure: float32 [256, 128, 1024], P('span', 'rows')
Inputs may be any that keep to these rules, and one draw needn't show every extreme that they name: owner is a span index.
All inputs are finite; a program needn't handle non-finite values.
Results may differ from a plain program's by a relative error of at most 0.00011.
Values sent between devices are 32-bit elements; how exact they have to be, the bound alone decides.
A program may use at most 64 MiB of HBM per device.

v0:
```python
import math
import jax
import jax.numpy as jnp
from jax import lax
from jax.sharding import Mesh
from jax.sharding import PartitionSpec as P

SWEEPS = 2
STEPS = 8
SPAN = ("span_0", "span_1", "span_2")
ROWS = ("rows_0", "rows_1")
LOWER_BOUND = 0.02
UPPER_BOUND = 2.0
HIGHEST = lax.Precision.HIGHEST


def spread(x, axes, root):
    x = jnp.where(lax.axis_index(axes) == root, x, jnp.zeros_like(x))
    for axis in axes:
        x = lax.psum(x, axis)
    return x


def in_one_piece(arrays, axis, split_dim, concat_dim, along):
    ends, at = ([], 0)
    for a in arrays[:-1]:
        at += a.shape[along]
        ends.append(at)
    both = jnp.concatenate(arrays, axis=along)
    return tuple(
        jnp.split(
            lax.all_to_all(both, axis, split_axis=split_dim, concat_axis=concat_dim, tiled=True),
            ends,
            axis=along,
        )
    )


def in_blocks(x, dim, size):
    before, after = (x.shape[:dim], x.shape[dim + 1 :])
    return jnp.moveaxis(x.reshape(*before, size, -1, *after), dim, 0)


def laid_out(parts, dim):
    dims = list(parts.shape[1:])
    dims[dim] *= parts.shape[0]
    return jnp.moveaxis(parts, 0, dim).reshape(dims)


def moved_by_axis(parts, axes, order):
    dims = [lax.axis_size(a) for a in axes]
    parts = parts.reshape(*dims, *parts.shape[1:])
    for k in order:
        parts = lax.all_to_all(parts, axes[k], split_axis=k, concat_axis=k, tiled=True)
    return parts.reshape(-1, *parts.shape[len(axes) :])


def core_and_chips(x, groups, order, split_dim, concat_dim):
    size = lax.axis_size(groups[0]) * lax.axis_size(groups[1])
    parts = in_blocks(x, split_dim, size)
    return laid_out(moved_by_axis(parts, groups, order), concat_dim)


def side_by_side(arrays, axis, dim, along):
    ends, at = ([], 0)
    for a in arrays[:-1]:
        at += a.shape[along]
        ends.append(at)
    both = jnp.concatenate(arrays, axis=along)
    return tuple(jnp.split(lax.all_gather(both, axis, axis=dim, tiled=True), ends, axis=along))


def reverse_bits(number, bit_count):
    result = number * 0
    for level in range(bit_count):
        result = result + number // 2**level % 2 * 2 ** (bit_count - 1 - level)
    return result


def apply_faces(planes, upper_rows, lower_rows, coeffs):
    left_face, right_face, top_face, bottom_face, diagonal = coeffs
    zero_col = jnp.zeros_like(planes[:, :, :1])
    left_cols = jnp.concatenate([zero_col, planes[:, :, :-1]], axis=2)
    right_cols = jnp.concatenate([planes[:, :, 1:], zero_col], axis=2)
    return (
        diagonal * planes
        - left_face * left_cols
        - right_face * right_cols
        - top_face * upper_rows
        - bottom_face * lower_rows
    )


def plain_operator(planes, coeffs):
    zero_row = jnp.zeros_like(planes[:, :1])
    upper_rows = jnp.concatenate([zero_row, planes[:, :-1]], axis=1)
    lower_rows = jnp.concatenate([planes[:, 1:], zero_row], axis=1)
    return apply_faces(planes, upper_rows, lower_rows, coeffs)


def chebyshev(rhs, coeffs, operator):
    center = (UPPER_BOUND + LOWER_BOUND) / 2.0
    half_width = (UPPER_BOUND - LOWER_BOUND) / 2.0
    sigma_ratio = center / half_width
    inverse_diag = 1.0 / coeffs[4]
    solution = jnp.zeros_like(rhs)
    residual = rhs
    for sweep_index in range(SWEEPS):
        ratio_now = 1.0 / sigma_ratio
        direction = residual * inverse_diag / center
        for step_index in range(STEPS):
            solution = solution + direction
            residual = residual - operator(direction, coeffs)
            ratio_next = 1.0 / (2.0 * sigma_ratio - ratio_now)
            direction = (
                ratio_next * ratio_now * direction
                + 2.0 * ratio_next / half_width * residual * inverse_diag
            )
            ratio_now = ratio_next
    return solution


def on_device(pressure_source, geometry, owner):
    span_count = lax.axis_size(SPAN)
    device = lax.axis_index(SPAN)
    bit_count = span_count.bit_length() - 1
    local_count, row_count, col_count = pressure_source.shape
    total_len = local_count * span_count
    plane = spread(geometry[0], SPAN, owner[0])
    west_face = plane[0]
    north_face = plane[1]
    volume = plane[2]
    merged = pressure_source.reshape((1, local_count * row_count, col_count))
    received = lax.all_to_all(merged, SPAN, split_axis=1, concat_axis=0, tiled=True)
    positions = jnp.arange(span_count, dtype=jnp.int32)
    freqs = reverse_bits(positions, bit_count)
    phase = (freqs[:, None] * positions[None, :] % span_count).astype(jnp.float32) * (
        -2.0 * math.pi / span_count
    )
    real_rows = jnp.einsum("rd,dtc->rtc", jnp.cos(phase), received, precision=HIGHEST)
    imag_rows = jnp.einsum("rd,dtc->rtc", jnp.sin(phase), received, precision=HIGHEST)
    real_back, imag_back = in_one_piece((real_rows, imag_rows), SPAN, 0, 1, 2)
    real_part = real_back.reshape(pressure_source.shape)
    imag_part = imag_back.reshape(pressure_source.shape)
    frequency = reverse_bits(device, bit_count)
    local_index = jnp.arange(local_count, dtype=jnp.int32)
    mode_index = frequency + span_count * local_index
    forward_phase = (mode_index[:, None] * local_index[None, :] % total_len).astype(jnp.float32) * (
        -2.0 * math.pi / total_len
    )
    forward_cos = jnp.cos(forward_phase)
    forward_sin = jnp.sin(forward_phase)
    spec_real = jnp.einsum("kj,jyc->kyc", forward_cos, real_part, precision=HIGHEST) - jnp.einsum(
        "kj,jyc->kyc", forward_sin, imag_part, precision=HIGHEST
    )
    spec_imag = jnp.einsum("kj,jyc->kyc", forward_sin, real_part, precision=HIGHEST) + jnp.einsum(
        "kj,jyc->kyc", forward_cos, imag_part, precision=HIGHEST
    )
    eigen = 2.0 - 2.0 * jnp.cos(mode_index.astype(jnp.float32) * (2.0 * math.pi / total_len))
    eigen_both = jnp.concatenate([eigen, eigen], axis=0)
    stacked = jnp.concatenate([spec_real, spec_imag], axis=0)
    rows_count = lax.axis_size(ROWS)
    row_device = lax.axis_index(ROWS)
    per_device = 2 * local_count // rows_count
    mine = core_and_chips(stacked, ("rows_0", "rows_1"), (1, 0), 0, 1)
    west_all, north_all, volume_all = side_by_side((west_face, north_face, volume), ROWS, 0, 1)
    east_all = jnp.concatenate([west_all[:, 1:], jnp.zeros_like(west_all[:, :1])], axis=1)
    south_all = jnp.concatenate([north_all[1:], jnp.zeros_like(north_all[:1])], axis=0)
    face_total = west_all + east_all + north_all + south_all
    eigen_mine = lax.dynamic_slice_in_dim(eigen_both, row_device * per_device, per_device)
    diagonal = face_total[None] + eigen_mine[:, None, None] * volume_all[None]
    coeffs = (west_all, east_all, north_all, south_all, diagonal)
    solved_mine = chebyshev(mine, coeffs, plain_operator)
    solved = lax.all_to_all(solved_mine, ROWS, split_axis=1, concat_axis=0, tiled=True)
    solved_real = solved[:local_count]
    solved_imag = solved[local_count:]
    inverse_cos = jnp.transpose(forward_cos) / local_count
    inverse_sin = -jnp.transpose(forward_sin) / local_count
    real_part = jnp.einsum("jk,kyc->jyc", inverse_cos, solved_real, precision=HIGHEST) - jnp.einsum(
        "jk,kyc->jyc", inverse_sin, solved_imag, precision=HIGHEST
    )
    imag_part = jnp.einsum("jk,kyc->jyc", inverse_sin, solved_real, precision=HIGHEST) + jnp.einsum(
        "jk,kyc->jyc", inverse_cos, solved_imag, precision=HIGHEST
    )
    merged_real = real_part.reshape((1, local_count * row_count, col_count))
    merged_imag = imag_part.reshape((1, local_count * row_count, col_count))
    recv_real, recv_imag = in_one_piece((merged_real, merged_imag), SPAN, 1, 0, 2)
    positions = jnp.arange(span_count, dtype=jnp.int32)
    freqs = reverse_bits(positions, bit_count)
    phase = (positions[:, None] * freqs[None, :] % span_count).astype(jnp.float32) * (
        2.0 * math.pi / span_count
    )
    gathered_rows = (
        jnp.einsum("ds,stc->dtc", jnp.cos(phase), recv_real, precision=HIGHEST)
        - jnp.einsum("ds,stc->dtc", jnp.sin(phase), recv_imag, precision=HIGHEST)
    ) / span_count
    pressure_back = lax.all_to_all(gathered_rows, SPAN, split_axis=0, concat_axis=1, tiled=True)
    return pressure_back.reshape(pressure_source.shape)


def solution(mesh):
    torus = Mesh(
        mesh.devices.reshape(2, 4, 8, 2, 2), ("span_0", "span_1", "span_2", "rows_0", "rows_1")
    )
    in_specs = (P(SPAN, ROWS, None), P(SPAN, None, ROWS, None), P())
    out_specs = P(SPAN, ROWS, None)
    return jax.shard_map(
        on_device, mesh=torus, in_specs=in_specs, out_specs=out_specs, check_vma=False
    )
```

profile of v0, /device:TPU:6, one launch (start us, length us, event | category | flops | bytes accessed | tf_op | source)
XLA Modules:
  0.0 380.6 jit_solution(5118960952709081886)
XLA Ops:
  6.5 2.5 reshape.288
  9.0 14.6 %all-to-all-start = ((f32[1,128,1024]{2,0,1:T(1,128)}), f32[1,128,1024]{2,0,1:T(1,128)S(1)}, u32[]{:S(2)}, u32[]{:S(2)}) async-start(f32[1,128,1024]{2,0,1:T(1,128)} %reshape.288), calls=%async_computation | async-start | bytes 1048576 | tf_op jit(solution)/shard_map/all_to_all | solution.py:134
  24.4 0.8 select_bitcast_fusion
  25.3 41.9 %all-reduce.66.cloned.1.call-done = f32[3,32,1024]{2,1,0:T(8,128)} async-done(((f32[3,32,1024]{2,1,0:T(8,128)}), f32[3,32,1024]{2,1,0:T(8,128)}) %all-reduce.66.cloned.1.call-update) | async-done | bytes 393232 | tf_op jit(solution)/shard_map/psum | solution.py:20
  67.2 1.2 reduce
  68.8 0.9 fusion.5
  69.7 0.9 fusion.7
  70.7 1.8 copy.21
  72.4 10.6 %all-to-all-start.1 = ((f32[64,2,2048]{2,1,0:T(2,128)}), f32[64,2,2048]{2,1,0:T(2,128)S(1)}, u32[]{:S(2)}, u32[]{:S(2)}) async-start(f32[64,2,2048]{2,1,0:T(2,128)} %copy.21), calls=%async_computation.1 | async-start | bytes 2097152 | tf_op jit(solution)/shard_map/all_to_all | solution.py:32
  83.1 35.4 %all-reduce.68.cloned.1.call-done = f32[3,32,1024]{2,1,0:T(8,128)} async-done(((f32[3,32,1024]{2,1,0:T(8,128)}), f32[3,32,1024]{2,1,0:T(8,128)}) %all-reduce.68.cloned.1.call-update) | async-done | bytes 393232 | tf_op jit(solution)/shard_map/psum | solution.py:20
  118.7 76.7 %all-reduce.70.cloned.1.call-done = f32[3,32,1024]{2,1,0:T(8,128)} async-done(((f32[3,32,1024]{2,1,0:T(8,128)}), f32[3,32,1024]{2,1,0:T(8,128)}) %all-reduce.70.cloned.1.call-update) | async-done | bytes 393232 | tf_op jit(solution)/shard_map/psum | solution.py:20
  195.4 1.1 slice_bitcast_fusion.2
  196.5 0.8 pad_maximum_fusion.3
  197.5 0.7 all_to_all.54
  198.3 1.3 fusion.11
  199.6 1.3 fusion.13
  200.9 1.3 convolution_subtract_fusion.1
  202.2 1.3 convolution_add_fusion.1
  203.8 0.6 reshape_reshape.3
  204.6 4.6 %all_to_all.70 = f32[2,2,2,32,1024]{4,2,0,3,1:T(2,128)S(1)} all-to-all(f32[2,2,2,32,1024]{4,2,0,3,1:T(2,128)S(1)} %copy.26), channel_id=1, replica_groups=mesh['span_0'=2,'span_1'=4,'span_2'=8,'rows_0'=2,'rows_1'=2] {'rows_1'}, dimensions={1} | all-to-all | bytes 2097152 | tf_op jit(solution)/shard_map/all_to_all | solution.py:54
  209.1 1.1 copy.27
  210.3 4.4 %all-to-all-start.3 = ((f32[2,2,2,32,1024]{4,2,1,3,0:T(2,128)}), f32[2,2,2,32,1024]{4,2,1,3,0:T(2,128)}, u32[]{:S(2)}, u32[]{:S(2)}) async-start(f32[2,2,2,32,1024]{4,2,1,3,0:T(2,128)} %copy.27), calls=%async_computation.3 | async-start | bytes 2097152 | tf_op jit(solution)/shard_map/all_to_all | solution.py:54
  214.9 13.3 %all-gather.2.cloned.1.call-done = f32[128,3072]{1,0:T(8,128)} async-done(((f32[32,3072]{1,0:T(8,128)}), f32[128,3072]{1,0:T(8,128)}) %all-gather.2.cloned.1.call-update) | async-done | bytes 1572880 | tf_op jit(solution)/shard_map/all_gather | solution.py:70
  228.2 1.2 slice.282
  229.4 1.3 slice.281
  231.0 3.6 all-to-all-done.3
  234.7 1.8 copy.28
  237.4 1.0 multiply_add_fusion.12
  239.1 2.1 multiply_add_fusion.11
  241.9 1.2 multiply_add_fusion.10
  243.7 1.2 multiply_add_fusion.9
  245.4 1.2 multiply_add_fusion.8
  247.2 1.2 multiply_add_fusion.7
  248.9 1.2 multiply_add_fusion.6
  250.7 1.2 broadcast_multiply_fusion
  252.5 1.1 multiply_add_fusion.5
  253.6 1.7 fusion.150
  255.3 1.9 fusion.151
  257.2 3.5 multiply_add_fusion.4
  261.4 1.2 multiply_add_fusion.3
  263.1 1.2 multiply_add_fusion.2
  264.9 1.2 multiply_add_fusion.1
  266.7 1.2 multiply_add_fusion
  268.3 1.2 fusion.141
  269.5 4.6 %add_add_fusion = f32[2,128,1024]{2,1,0:T(8,128)S(1)} fusion(f32[2,127,1024]{2,1,0:T(8,128)} %get-tuple-element.38, f32[2,127,1024]{2,1,0:T(8,128)S(1)} %get-tuple-element.37, f32[2,128,1023]{2,1,0:T(8,128)S(1)} %get-tuple-element.36, f32[2,128,1023]{2,1,0:T(8,128)S(1)} %get-tuple-element.35, f32[2,128,1024]{2,1,0:T(8,128)S(1)} %get-tuple-element.7, ...), kind=kLoop, calls=%fused_computation.11 | loop fusion | flops 15204352 | bytes 27226120 | tf_op jit(solution)/shard_map/add | solution.py:112
  274.2 0.8 copy.29
  275.0 17.0 %all_to_all.71 = f32[2,128,1024]{2,0,1:T(2,128)S(1)} all-to-all(f32[2,128,1024]{2,0,1:T(2,128)S(1)} %copy.29), channel_id=1, replica_groups=mesh['span_0'=2,'span_1'=4,'span_2'=8,'rows_0'=2,'rows_1'=2] {'rows_0','..., dimensions={1} | all-to-all | bytes 2097152 | tf_op jit(solution)/shard_map/all_to_all | solution.py:174
  292.5 0.4 copy.31
  292.9 0.5 slice.275
  293.3 1.0 fusion.45
  294.4 1.0 fusion.53
  295.4 0.4 copy.32
  295.8 0.5 slice.277
  296.3 1.0 convolution_subtract_fusion
  297.3 1.0 convolution_add_fusion
  299.1 1.1 copy.35
  300.2 43.1 %all_to_all.72 = f32[1,128,2048]{2,0,1:T(1,128)S(1)} all-to-all(f32[1,128,2048]{2,0,1:T(1,128)S(1)} %copy.35), channel_id=1, replica_groups=mesh['span_0'=2,'span_1'=4,'span_2'=8,'rows_0'=2,'rows_1'=2] {'span_0','..., dimensions={1} | all-to-all | bytes 2097152 | tf_op jit(solution)/shard_map/all_to_all | solution.py:32
  343.2 2.5 reduce.1
  345.7 0.6 all_to_all.61
  346.4 0.8 fusion.3
  347.2 0.8 fusion
  348.0 0.4 copy.38
  348.5 24.2 %all_to_all.73 = f32[64,2,1024]{2,1,0:T(2,128)S(1)} all-to-all(f32[64,2,1024]{2,1,0:T(2,128)S(1)} %copy.38), channel_id=1, replica_groups=mesh['span_0'=2,'span_1'=4,'span_2'=8,'rows_0'=2,'rows_1'=2] {'span_0','..., dimensions={0} | all-to-all | bytes 1048576 | tf_op jit(solution)/shard_map/all_to_all | solution.py:197
  372.7 1.2 reshape.295
  (59 shorter events, 11.4 us)
Async XLA Ops:
  6.5 17.9 %copy-start.1 = (f32[1,3,32,1024]{3,2,1,0:T(8,128)S(1)}, f32[1,3,32,1024]{3,2,1,0:T(8,128)}, u32[]{:S(2)}) copy-start(f32[1,3,32,1024]{3,2,1,0:T(8,128)} %param.4) | copy-start | bytes 1179652
  9.0 58.2 %all-to-all-start = ((f32[1,128,1024]{2,0,1:T(1,128)}), f32[1,128,1024]{2,0,1:T(1,128)S(1)}, u32[]{:S(2)}, u32[]{:S(2)}) async-start(f32[1,128,1024]{2,0,1:T(1,128)} %reshape.288), calls=%async_computation | async-start | bytes 1048576 | tf_op jit(solution)/shard_map/all_to_all | solution.py:134
  23.7 43.5 %all-reduce.66.cloned.1.call-start = ((), (), s32[]{:S(2)}) async-start(), calls=%async_computation.7 | async-start | bytes 786432 | tf_op jit(solution)/shard_map/psum | solution.py:20
  25.2 93.2 %all-reduce.68.cloned.1.call-start = ((), (), s32[]{:S(2)}) async-start(), calls=%async_computation.8 | async-start | bytes 786432 | tf_op jit(solution)/shard_map/psum | solution.py:20
  72.4 125.0 %all-to-all-start.1 = ((f32[64,2,2048]{2,1,0:T(2,128)}), f32[64,2,2048]{2,1,0:T(2,128)S(1)}, u32[]{:S(2)}, u32[]{:S(2)}) async-start(f32[64,2,2048]{2,1,0:T(2,128)} %copy.21), calls=%async_computation.1 | async-start | bytes 2097152 | tf_op jit(solution)/shard_map/all_to_all | solution.py:32
  83.0 112.4 %all-reduce.70.cloned.1.call-start = ((), (), s32[]{:S(2)}) async-start(), calls=%async_computation.9 | async-start | bytes 786432 | tf_op jit(solution)/shard_map/psum | solution.py:20
  118.5 109.7 %all-gather.2.cloned.1.call-start = ((), (), s32[]{:S(2)}) async-start(), calls=%async_computation.10 | async-start | bytes 1966080 | tf_op jit(solution)/shard_map/all_gather | solution.py:70
  210.3 24.4 %all-to-all-start.3 = ((f32[2,2,2,32,1024]{4,2,1,3,0:T(2,128)}), f32[2,2,2,32,1024]{4,2,1,3,0:T(2,128)}, u32[]{:S(2)}, u32[]{:S(2)}) async-start(f32[2,2,2,32,1024]{4,2,1,3,0:T(2,128)} %copy.27), calls=%async_computation.3 | async-start | bytes 2097152 | tf_op jit(solution)/shard_map/all_to_all | solution.py:54
  228.2 2.5 copy-start
Sparse Core Ops, SparseCore 0:
  27.1 40.0 all-reduce.65
  69.6 48.7 all-reduce.67
  120.8 74.6 all-reduce.69
  197.4 30.7 all-gather.1
where the time goes:
time: 387 us; the launch traced here: 381 us
  waiting for transfers between devices  171 us (44%)
  blocking collectives  88.9 us (23%)
  local copies, waits for them, and re-layouts  32.6 us (8%)
  other arithmetic  30.6 us (8%)
  starting transfers between devices  30 us (8%)
  between operations  14.8 us (4%)
  matrix products  12.8 us (3%)
    psum x3, waiting for transfers between devices, spread(): x = lax.psum(x, axis)  154 us
    all_to_all x1, blocking collectives, in_one_piece(): lax.all_to_all(both, axis, split_axis=split_dim, concat_axis=concat_dim,...  43.1 us
    all_to_all x1, blocking collectives, on_device(): lax.all_to_all(gathered_rows, SPAN, split_axis=0, concat_axis=1, tiled=True)  24.2 us
    add x13, other arithmetic, chebyshev(): ratio_next * ratio_now * direction  18.3 us
    all_to_all x1, blocking collectives, on_device(): lax.all_to_all(solved_mine, ROWS, split_axis=1, concat_axis=0, tiled=True)  17 us
    all_to_all x1, starting transfers between devices, on_device(): lax.all_to_all(merged, SPAN, split_axis=1, concat_axis=0, tiled=True)  14.6 us
    all_gather x1, waiting for transfers between devices, side_by_side(): lax.all_gather(both, axis, axis=dim, tiled=True)  13.3 us
    all_to_all x1, starting transfers between devices, in_one_piece(): lax.all_to_all(both, axis, split_axis=split_dim, concat_axis=concat_dim,...  10.6 us
  transfers between devices with their start and end apart: 7, of which 5 were waited for; matrix products, arithmetic and copies ran while one was open for 5% of the time, Pallas kernels for 0%

commit v1 on v0

--- a/solution.py
+++ b/solution.py
@@ -17,7 +17,7 @@
 def spread(x, axes, root):
     x = jnp.where(lax.axis_index(axes) == root, x, jnp.zeros_like(x))
     for axis in axes:
-        x = lax.psum(x, axis)
+        x = jnp.sum(lax.all_gather(x, axis), axis=0)
     return x
 
 

time: 387 us -> 323 us (0.83)
  waiting for transfers between devices: 171 us -> 100 us
  blocking collectives: 88.9 us -> 101 us
  starting transfers between devices: 30 us -> 22.5 us
  other arithmetic: 30.6 us -> 36 us
    psum x3 -> x0, waiting for transfers between devices: 154 us -> none  [spread(): x = lax.psum(x, axis)]
    all_gather x0 -> x2, waiting for transfers between devices: none -> 51.9 us  [spread(): x = jnp.sum(lax.all_gather(x, axis), axis=0)]
    all_to_all x1, waiting for transfers between devices: 0.01 us -> 25.3 us  [on_device(): lax.all_to_all(merged, SPAN, split_axis=1, concat_axis=0, tiled=True)]
    all_gather x1, waiting for transfers between devices: 13.3 us -> 0.02 us  [side_by_side(): lax.all_gather(both, axis, axis=dim, tiled=True)]
    all_gather x0 -> x1, blocking collectives: none -> 13 us  [spread(): x = jnp.sum(lax.all_gather(x, axis), axis=0)]
    all_to_all x1, waiting for transfers between devices: 3.65 us -> 14 us  [moved_by_axis(): lax.all_to_all(parts, axes[k], split_axis=k, concat_axis=k, tiled=True)]
    all_to_all x1, waiting for transfers between devices: 0.01 us -> 8.95 us  [in_one_piece(): lax.all_to_all(both, axis, split_axis=split_dim, concat_axis=concat_dim,...]
    reduce_sum x0 -> x3, other arithmetic: none -> 5.26 us  [spread(): x = jnp.sum(lax.all_gather(x, axis), axis=0)]
  transfers between devices with their start and end apart: 7 -> 6, of which waited for: 5 -> 5; matrix products, arithmetic and copies ran while one was open for 5% -> 6% of each run, Pallas kernels for 0% -> 0%
where the time goes in v1:
time: 323 us; the launch traced here: 316 us
  blocking collectives  101 us (31%)
  waiting for transfers between devices  100 us (31%)
  other arithmetic  36 us (11%)
  local copies, waits for them, and re-layouts  29.4 us (9%)
  starting transfers between devices  22.5 us (7%)
  between operations  14.8 us (5%)
  matrix products  12.8 us (4%)
    all_gather x2, waiting for transfers between devices, spread(): x = jnp.sum(lax.all_gather(x, axis), axis=0)  51.9 us
    all_to_all x1, blocking collectives, in_one_piece(): lax.all_to_all(both, axis, split_axis=split_dim, concat_axis=concat_dim,...  41.7 us
    all_to_all x1, waiting for transfers between devices, on_device(): lax.all_to_all(merged, SPAN, split_axis=1, concat_axis=0, tiled=True)  25.3 us
    all_to_all x1, blocking collectives, on_device(): lax.all_to_all(gathered_rows, SPAN, split_axis=0, concat_axis=1, tiled=True)  24.2 us
    add x13, other arithmetic, chebyshev(): ratio_next * ratio_now * direction  18.9 us
    all_to_all x1, blocking collectives, on_device(): lax.all_to_all(solved_mine, ROWS, split_axis=1, concat_axis=0, tiled=True)  17 us
    all_to_all x1, waiting for transfers between devices, moved_by_axis(): lax.all_to_all(parts, axes[k], split_axis=k, concat_axis=k, tiled=True)  14 us
    all_gather x1, blocking collectives, spread(): x = jnp.sum(lax.all_gather(x, axis), axis=0)  13 us
  transfers between devices with their start and end apart: 6, of which 5 were waited for; matrix products, arithmetic and copies ran while one was open for 6% of the time, Pallas kernels for 0%

profile of v1, /device:TPU:6, one launch (start us, length us, event | category | flops | bytes accessed | tf_op | source)
XLA Modules:
  0.0 316.3 jit_solution(6916310463067786564)
XLA Ops:
  7.2 13.0 %all_gather.19 = f32[2,3,32,1024]{3,2,1,0:T(8,128)S(1)} all-gather(f32[1,3,32,1024]{3,2,1,0:T(8,128)S(1)} %broadcast_select_fusion), channel_id=1, replica_groups=mesh['span_0'=2,'span_1'=4,'span_2'=8,'rows_0'=2,'rows_1'=2] {'span_0'}, dimensions={0}, use_global_device_ids=true | all-gather | bytes 1179648 | tf_op jit(solution)/shard_map/all_gather | solution.py:20
  20.3 0.8 reduce_sum.27
  21.1 31.0 %all-gather.8.cloned.1.call-done = f32[12,32,1024]{2,1,0:T(8,128)} async-done(((f32[3,32,1024]{2,1,0:T(8,128)}), f32[12,32,1024]{2,1,0:T(8,128)}) %all-gather.8.cloned.1.call-update) | async-done | bytes 1572880 | tf_op jit(solution)/shard_map/all_gather | solution.py:20
  52.2 2.3 reduce_sum.28
  54.5 1.4 reshape.285
  55.9 12.9 %all-to-all-start = ((f32[1,128,1024]{2,0,1:T(1,128)}), f32[1,128,1024]{2,0,1:T(1,128)S(1)}, u32[]{:S(2)}, u32[]{:S(2)}) async-start(f32[1,128,1024]{2,0,1:T(1,128)} %reshape.285), calls=%async_computation | async-start | bytes 1048576 | tf_op jit(solution)/shard_map/all_to_all | solution.py:134
  68.8 25.3 %all-to-all-done = f32[1,128,1024]{2,0,1:T(1,128)S(1)} async-done(((f32[1,128,1024]{2,0,1:T(1,128)}), f32[1,128,1024]{2,0,1:T(1,128)S(1)}, u32[]{:S(2)}, u32[]{:S(2)}) %all-to-all-start) | async-done | bytes 524320 | tf_op jit(solution)/shard_map/all_to_all | solution.py:134
  94.2 1.2 reduce
  95.7 0.9 fusion.5
  96.6 0.9 fusion.7
  97.6 1.8 copy.21
  99.4 5.8 %all-to-all-start.1 = ((f32[64,2,2048]{2,1,0:T(2,128)}), f32[64,2,2048]{2,1,0:T(2,128)S(1)}, u32[]{:S(2)}, u32[]{:S(2)}) async-start(f32[64,2,2048]{2,1,0:T(2,128)} %copy.21), calls=%async_computation.1 | async-start | bytes 2097152 | tf_op jit(solution)/shard_map/all_to_all | solution.py:32
  105.4 20.9 %all-gather.10.cloned.1.call-done = f32[24,32,1024]{2,1,0:T(8,128)} async-done(((f32[3,32,1024]{2,1,0:T(8,128)}), f32[24,32,1024]{2,1,0:T(8,128)}) %all-gather.10.cloned.1.call-update) | async-done | bytes 3145744 | tf_op jit(solution)/shard_map/all_gather | solution.py:20
  126.3 2.2 reduce_sum.29
  128.5 0.8 pad_maximum_fusion.3
  129.4 8.9 %all-to-all-done.1 = f32[64,2,2048]{2,1,0:T(2,128)S(1)} async-done(((f32[64,2,2048]{2,1,0:T(2,128)}), f32[64,2,2048]{2,1,0:T(2,128)S(1)}, u32[]{:S(2)}, u32[]{:S(2)}) %all-to-all-start.1) | async-done | bytes 1048608 | tf_op jit(solution)/shard_map/all_to_all | solution.py:32
  138.4 0.7 all_to_all.54
  139.2 1.3 fusion.11
  140.5 1.3 fusion.13
  141.8 1.3 convolution_subtract_fusion.1
  143.2 1.3 convolution_add_fusion.1
  144.7 0.6 reshape_reshape.3
  145.5 4.6 %all_to_all.70 = f32[2,2,2,32,1024]{4,2,0,3,1:T(2,128)S(1)} all-to-all(f32[2,2,2,32,1024]{4,2,0,3,1:T(2,128)S(1)} %copy.26), channel_id=1, replica_groups=mesh['span_0'=2,'span_1'=4,'span_2'=8,'rows_0'=2,'rows_1'=2] {'rows_1'}, dimensions={1} | all-to-all | bytes 2097152 | tf_op jit(solution)/shard_map/all_to_all | solution.py:54
  150.1 1.1 copy.27
  151.2 3.6 %all-to-all-start.3 = ((f32[2,2,2,32,1024]{4,2,1,3,0:T(2,128)}), f32[2,2,2,32,1024]{4,2,1,3,0:T(2,128)S(1)}, u32[]{:S(2)}, u32[]{:S(2)}) async-start(f32[2,2,2,32,1024]{4,2,1,3,0:T(2,128)} %copy.27), calls=%async_computation.3 | async-start | bytes 2097152 | tf_op jit(solution)/shard_map/all_to_all | solution.py:54
  155.0 14.0 %all-to-all-done.3 = f32[2,2,2,32,1024]{4,2,1,3,0:T(2,128)S(1)} async-done(((f32[2,2,2,32,1024]{4,2,1,3,0:T(2,128)}), f32[2,2,2,32,1024]{4,2,1,3,0:T(2,128)S(1)}, u32[]{:S(2)}, u32[]{:S(2)}) %all-to-all-start.3) | async-done | bytes 1048608 | tf_op jit(solution)/shard_map/all_to_all | solution.py:54
  169.0 0.6 copy.28
  169.6 1.2 slice.282
  170.8 1.3 slice.281
  172.1 0.5 fusion.137
  173.5 1.0 multiply_add_fusion.12
  175.2 2.1 multiply_add_fusion.11
  178.0 1.3 multiply_add_fusion.10
  179.9 1.3 multiply_add_fusion.9
  181.9 1.3 multiply_add_fusion.8
  183.8 1.3 multiply_add_fusion.7
  185.8 1.3 multiply_add_fusion.6
  187.7 1.3 broadcast_multiply_fusion
  189.7 1.0 multiply_add_fusion.5
  190.7 1.7 fusion.150
  192.5 1.9 fusion.151
  194.4 3.6 %multiply_add_fusion.4 = (f32[2,128,1024]{2,1,0:T(8,128)S(1)}, f32[2,128,1024]{2,1,0:T(8,128)S(1)}) fusion(f32[2,128,1024]{2,1,0:T(8,128)S(1)} %multiply_add_fusion.5, f32[128,1024]{1,0:T(8,128)S(1)} %get-tuple-element.29, f32[2]{0:T(128)S(1)} %dynamic_slice.3, f32[128,1024]{1,0:T(8,128)S(1)} %get-tuple-element.28, f32[2,127,1024]{2,1,0:T(8,128)} %get-tuple-element.58, ...), kind=kLoop, calls=%fused_computation.20 | loop fusion | flops 7602176 | bytes 15691784 | tf_op jit(solution)/shard_map/add | solution.py:116
  198.5 1.1 multiply_add_fusion.3
  200.3 1.1 multiply_add_fusion.2
  202.0 1.2 multiply_add_fusion.1
  203.7 1.2 multiply_add_fusion
  205.4 1.2 fusion.141
  206.6 4.6 %add_add_fusion = f32[2,128,1024]{2,1,0:T(8,128)S(1)} fusion(f32[2,127,1024]{2,1,0:T(8,128)} %get-tuple-element.38, f32[2,127,1024]{2,1,0:T(8,128)S(1)} %get-tuple-element.37, f32[2,128,1023]{2,1,0:T(8,128)S(1)} %get-tuple-element.36, f32[2,128,1023]{2,1,0:T(8,128)S(1)} %get-tuple-element.35, f32[2,128,1024]{2,1,0:T(8,128)S(1)} %get-tuple-element.7, ...), kind=kLoop, calls=%fused_computation.11 | loop fusion | flops 15204352 | bytes 27226120 | tf_op jit(solution)/shard_map/add | solution.py:112
  211.2 0.8 copy.29
  212.1 17.0 %all_to_all.71 = f32[2,128,1024]{2,0,1:T(2,128)S(1)} all-to-all(f32[2,128,1024]{2,0,1:T(2,128)S(1)} %copy.29), channel_id=1, replica_groups=mesh['span_0'=2,'span_1'=4,'span_2'=8,'rows_0'=2,'rows_1'=2] {'rows_0','..., dimensions={1} | all-to-all | bytes 2097152 | tf_op jit(solution)/shard_map/all_to_all | solution.py:174
  229.9 0.5 slice.275
  230.4 1.0 fusion.45
  231.4 1.0 fusion.53
  232.9 0.5 slice.277
  233.3 1.0 convolution_subtract_fusion
  234.4 1.0 convolution_add_fusion
  236.1 1.1 copy.35
  237.2 41.7 %all_to_all.72 = f32[1,128,2048]{2,0,1:T(1,128)S(1)} all-to-all(f32[1,128,2048]{2,0,1:T(1,128)S(1)} %copy.35), channel_id=1, replica_groups=mesh['span_0'=2,'span_1'=4,'span_2'=8,'rows_0'=2,'rows_1'=2] {'span_0','..., dimensions={1} | all-to-all | bytes 2097152 | tf_op jit(solution)/shard_map/all_to_all | solution.py:32
  278.9 2.5 reduce.1
  281.4 0.6 all_to_all.61
  282.2 0.8 fusion.3
  282.9 0.8 fusion
  284.2 24.2 %all_to_all.73 = f32[64,2,1024]{2,1,0:T(2,128)S(1)} all-to-all(f32[64,2,1024]{2,1,0:T(2,128)S(1)} %copy.38), channel_id=1, replica_groups=mesh['span_0'=2,'span_1'=4,'span_2'=8,'rows_0'=2,'rows_1'=2] {'span_0','..., dimensions={0} | all-to-all | bytes 1048576 | tf_op jit(solution)/shard_map/all_to_all | solution.py:197
  308.4 1.2 reshape.292
  (60 shorter events, 12.4 us)
Async XLA Ops:
  6.5 45.6 %all-gather.8.cloned.1.call-start = ((), (), s32[]{:S(2)}) async-start(), calls=%async_computation.8 | async-start | bytes 1966080 | tf_op jit(solution)/shard_map/all_gather | solution.py:20
  21.1 33.4 %copy-start.1 = (f32[4,32,1024]{2,1,0:T(8,128)S(1)}, f32[4,32,1024]{2,1,0:T(8,128)}, u32[]{:S(2)}) copy-start(f32[4,32,1024]{2,1,0:T(8,128)} %param.3) | copy-start | bytes 1572868
  21.1 105.2 %all-gather.10.cloned.1.call-start = ((), (), s32[]{:S(2)}) async-start(), calls=%async_computation.9 | async-start | bytes 3538944 | tf_op jit(solution)/shard_map/all_gather | solution.py:20
  55.9 38.3 %all-to-all-start = ((f32[1,128,1024]{2,0,1:T(1,128)}), f32[1,128,1024]{2,0,1:T(1,128)S(1)}, u32[]{:S(2)}, u32[]{:S(2)}) async-start(f32[1,128,1024]{2,0,1:T(1,128)} %reshape.285), calls=%async_computation | async-start | bytes 1048576 | tf_op jit(solution)/shard_map/all_to_all | solution.py:134
  99.4 39.0 %all-to-all-start.1 = ((f32[64,2,2048]{2,1,0:T(2,128)}), f32[64,2,2048]{2,1,0:T(2,128)S(1)}, u32[]{:S(2)}, u32[]{:S(2)}) async-start(f32[64,2,2048]{2,1,0:T(2,128)} %copy.21), calls=%async_computation.1 | async-start | bytes 2097152 | tf_op jit(solution)/shard_map/all_to_all | solution.py:32
  105.2 64.4 %all-gather.6.cloned.1.call-start = ((), (), s32[]{:S(2)}) async-start(), calls=%async_computation.7 | async-start | bytes 1966080 | tf_op jit(solution)/shard_map/all_gather | solution.py:70
  151.2 17.8 %all-to-all-start.3 = ((f32[2,2,2,32,1024]{4,2,1,3,0:T(2,128)}), f32[2,2,2,32,1024]{4,2,1,3,0:T(2,128)S(1)}, u32[]{:S(2)}, u32[]{:S(2)}) async-start(f32[2,2,2,32,1024]{4,2,1,3,0:T(2,128)} %copy.27), calls=%async_computation.3 | async-start | bytes 2097152 | tf_op jit(solution)/shard_map/all_to_all | solution.py:54
  169.6 2.5 copy-start
Sparse Core Ops, SparseCore 0:
  21.2 30.8 all-gather.7
  54.6 71.6 all-gather.9
  129.4 26.9 all-gather.5
